TPU v7x, 512 devices: a whole 4x8x8 slice. The times are simulated.
512 devices in a mesh: section: 32 (over y_hi, z, core), expert: 16 (over y_lo, x).
Axes of the slice: x: 4, y: 8 (y_hi: 2, y_lo: 4; y = y_hi * 4 + y_lo), z: 8, core: 2. Of those that a mesh axis runs over, the one named last changes fastest.
Arguments:
- acts: bfloat16 [32, 2048, 2048], P('section', 'expert'), may hold values from -6 to 6
- routes: int32 [32, 2048, 2], P('section', 'expert'), may hold values from 0 to 3, all different within a row; in each aligned block of 128 rows (0 to 127, 128 to 255, ..., all dimensions but the last counted through in order) at most 96 rows name the same one
- gates: float32 [32, 2048, 2], P('section', 'expert'), may hold values from 0.2 to 1
- norm_gain: float32 [32, 2048], P('section'), may hold values from 0.5 to 1.5
- gate_w: bfloat16 [32, 2048, 4096], P('section', None, 'expert'), may hold values from -0.125 to 0.125
- up_w: bfloat16 [32, 2048, 4096], P('section', None, 'expert'), may hold values from -0.125 to 0.125
- down_w: bfloat16 [32, 4096, 2048], P('section', 'expert'), may hold values from -0.1875 to 0.1875
Outputs:
- result: bfloat16 [32, 2048, 2048], P('section', 'expert')
Inputs may be any that keep to these rules, and one draw needn't show every extreme that they name: `routes`: each token names 2 different experts. Among the rows of one device, no expert is named by more than 96 tokens, and in every draw some expert is named by exactly 96.
All inputs are finite; a program needn't handle non-finite values.
Results may differ from a plain program's by a relative error of at most 0.005.
Values may be sent and summed in bfloat16 or wider, within the bound.
A program may use at most 64 MiB of HBM per device.

v0:
```python
import jax
import jax.numpy as jnp
from jax import lax
from jax.sharding import PartitionSpec as P

NEXP = 4
CAP = 96


def shifted(value, axis, steps):
    count = lax.axis_size(axis)
    pairs = [(source, (source + steps) % count) for source in range(count)]
    return lax.ppermute(value, axis, pairs)


def expert_rows(rows, wgate, wup, wdown):
    gpart = jnp.einsum("scd,dh->sch", rows, wgate, preferred_element_type=jnp.float32)
    upart = jnp.einsum("scd,dh->sch", rows, wup, preferred_element_type=jnp.float32)
    hidden = (jax.nn.silu(gpart) * upart).astype(jnp.bfloat16)
    return jnp.einsum("sch,hd->scd", hidden, wdown, preferred_element_type=jnp.float32).astype(
        jnp.bfloat16
    )


def local(acts, routes, gates, norm_gain, gate_w, up_w, down_w):
    arrived = shifted(acts, "section", 1)[0]
    ids = routes[0]
    weights = gates[0]
    gain = norm_gain[0]
    wgate = gate_w[0]
    wup = up_w[0]
    wdown = down_w[0]
    hsplit = lax.axis_size("expert") // NEXP
    tok_count = ids.shape[0]
    chosen = (ids[:, :, None] == jnp.arange(NEXP, dtype=jnp.int32)[None, None, :]).astype(jnp.int32)
    member = jnp.sum(chosen, axis=1)
    gate_of = jnp.sum(weights[:, :, None] * chosen.astype(jnp.float32), axis=1)
    slot_rank = jnp.cumsum(member, axis=0) - 1
    slots = jnp.arange(CAP, dtype=jnp.int32)
    place = (slot_rank.T[:, None, :] == slots[None, :, None]) & (member.T[:, None, :] > 0)
    place_bf = place.astype(jnp.bfloat16)
    xf = arrived.astype(jnp.float32)
    scale = lax.rsqrt(jnp.mean(xf * xf, axis=1, keepdims=True) + 1e-06)
    normed = (xf * scale * gain[None, :]).astype(jnp.bfloat16)
    packed = jnp.einsum("gct,td->gcd", place_bf, normed, preferred_element_type=jnp.float32).astype(
        jnp.bfloat16
    )
    outgoing = jnp.repeat(packed, hsplit, axis=0)
    received = lax.all_to_all(outgoing, "expert", split_axis=0, concat_axis=0, tiled=True)
    returned = lax.all_to_all(
        expert_rows(received, wgate, wup, wdown), "expert", split_axis=0, concat_axis=0, tiled=True
    )
    shards = returned.reshape(NEXP, hsplit, CAP, returned.shape[-1])
    per_expert = jnp.einsum("gct,ghcd->gtd", place_bf, shards, preferred_element_type=jnp.float32)
    contrib = jnp.sum(per_expert * gate_of.T[:, :, None], axis=0)
    result = (xf + contrib).astype(jnp.bfloat16)
    return result.reshape(1, tok_count, result.shape[-1])


def solution(mesh):
    in_specs = (
        P("section", "expert", None),
        P("section", "expert", None),
        P("section", "expert", None),
        P("section", None),
        P("section", None, "expert"),
        P("section", None, "expert"),
        P("section", "expert", None),
    )
    out_specs = P("section", "expert", None)
    return jax.shard_map(local, mesh=mesh, in_specs=in_specs, out_specs=out_specs, check_vma=False)
```

profile of v0, /device:TPU:208, one launch (start us, length us, event | category | flops | bytes accessed | tf_op | source)
XLA Modules:
  0.0 328.6 jit_solution(6189890254812739712)
XLA Ops:
  0.0 0.0 copy-start
  0.0 2.0 collective-permute-start
  2.1 0.7 convert_reduce_fusion.1
  2.7 0.1 copy.12
  2.9 0.2 reduce_window_sum.11
  3.0 0.1 copy.13
  3.1 7.7 %collective-permute-done = bf16[1,128,2048]{2,1,0:T(8,128)(2,1)S(1)} collective-permute-done((bf16[1,128,2048]{2,1,0:T(8,128)(2,1)}, bf16[1,128,2048]{2,1,0:T(8,128)(2,1)S(1)}, u32[]{:S(2)}, u32[]{:S(2)}) %collective-permute-start) | collective-permute-done | bytes 524320 | tf_op jit(solution)/shard_map/ppermute | solution.py:13
  10.8 0.2 fusion.2
  11.0 1.3 convolution_convert_fusion.1
  12.4 0.8 broadcast_in_dim.2
  13.2 0.0 copy-start.4
  13.2 147.7 %all_to_all.10 = bf16[16,96,2048]{2,1,0:T(8,128)(2,1)S(1)} all-to-all(bf16[16,96,2048]{2,1,0:T(8,128)(2,1)S(1)} %bitcast.48), channel_id=1, replica_groups=mesh['section'=32,'expert'=16] {'expert'}, dimensions={0} | all-to-all | bytes 12582912 | tf_op jit(solution)/shard_map/all_to_all | solution.py:49
  160.9 0.0 copy-start.1
  160.9 2.7 copy-done.1
  163.6 0.0 copy-done.4
  163.6 0.0 copy-start.5
  163.6 3.0 fusion.9
  166.6 0.0 copy-done
  166.6 0.0 copy-done.5
  166.6 12.3 %convolution_convert_fusion = bf16[16,96,2048]{2,1,0:T(8,128)(2,1)} fusion(f32[16,96,256]{2,1,0:T(8,128)} %fusion.9, bf16[16,96,2048]{2,1,0:T(8,128)(2,1)} %copy-done.1, bf16[1,256,2048]{2,1,0:T(8,128)(2,1)S(1)} %copy-done, bf16[1,2048,256]{2,1,0:T(8,128)(2,1)S(1)} %copy-done.5), kind=kOutput, calls=%fused_computation.1 | convolution fusion | flops 3226730496 | bytes 16252928 | tf_op jit(solution)/shard_map/sch,hd->scd/dot_general | solution.py:20
  178.9 0.0 copy-start.2
  178.9 0.0 copy-start.3
  178.9 5.1 %all-to-all-start.1 = ((bf16[16,96,2048]{2,1,0:T(8,128)(2,1)}), bf16[16,96,2048]{2,1,0:T(8,128)(2,1)}, u32[]{:S(2)}, u32[]{:S(2)}) async-start(bf16[16,96,2048]{2,1,0:T(8,128)(2,1)} %convolution_convert_fusion), calls=%async_computation.1 | async-start | bytes 12582912 | tf_op jit(solution)/shard_map/all_to_all | solution.py:50
  184.1 0.0 copy-done.2
  184.1 0.0 copy-done.3
  184.1 138.5 %all-to-all-done.1 = bf16[16,96,2048]{2,1,0:T(8,128)(2,1)} async-done(((bf16[16,96,2048]{2,1,0:T(8,128)(2,1)}), bf16[16,96,2048]{2,1,0:T(8,128)(2,1)}, u32[]{:S(2)}, u32[]{:S(2)}) %all-to-all-start.1) | async-done | bytes 6291488 | tf_op jit(solution)/shard_map/all_to_all | solution.py:50
  322.6 4.2 %convert_reduce_fusion = bf16[4,96,2048]{2,1,0:T(8,128)(2,1)S(1)} fusion(bf16[16,96,2048]{2,1,0:T(8,128)(2,1)} %all-to-all-done.1), kind=kLoop, calls=%fused_computation | loop fusion | flops 5505024 | bytes 7864320 | tf_op jit(solution)/shard_map/gct,ghcd->gtd/reduce_sum | solution.py:54
  326.8 0.8 multiply_reduce_fusion
  327.6 0.9 fusion.5
  (4 shorter events, 0.0 us)
Async XLA Ops:
  0.0 166.6 %copy-start = (bf16[1,256,2048]{2,1,0:T(8,128)(2,1)S(1)}, bf16[1,256,2048]{2,1,0:T(8,128)(2,1)}, u32[]{:S(2)}) copy-start(bf16[1,256,2048]{2,1,0:T(8,128)(2,1)} %param.13) | copy-start | bytes 3145732
  0.0 10.8 %collective-permute-start = (bf16[1,128,2048]{2,1,0:T(8,128)(2,1)}, bf16[1,128,2048]{2,1,0:T(8,128)(2,1)S(1)}, u32[]{:S(2)}, u32[]{:S(2)}) collective-permute-start(bf16[1,128,2048]{2,1,0:T(8,128)(2,1)} %param.7), channel_id=1, source_target_pairs={{0,16},{16,32},{32,48},{48,64},{64,80},{80,96},{96,112},{112,128},... | collective-permute-start | bytes 1572872 | tf_op jit(solution)/shard_map/ppermute | solution.py:13
  13.2 150.4 %copy-start.4 = (bf16[1,2048,256]{2,1,0:T(8,128)(2,1)S(1)}, bf16[1,2048,256]{2,1,0:T(8,128)(2,1)}, u32[]{:S(2)}) copy-start(bf16[1,2048,256]{2,1,0:T(8,128)(2,1)} %param.11) | copy-start | bytes 3145732
  160.9 2.7 copy-start.1
  163.6 3.0 copy-start.5
  178.9 5.1 %copy-start.2 = (s32[1,128,2]{1,2,0:T(2,128)S(1)}, s32[1,128,2]{1,2,0:T(2,128)}, u32[]{:S(2)}) copy-start(s32[1,128,2]{1,2,0:T(2,128)} %param.8) | copy-start | bytes 3076
  178.9 5.2 %copy-start.3 = (f32[1,128,2]{1,2,0:T(2,128)S(1)}, f32[1,128,2]{1,2,0:T(2,128)}, u32[]{:S(2)}) copy-start(f32[1,128,2]{1,2,0:T(2,128)} %param.9) | copy-start | bytes 3076
  178.9 143.7 %all-to-all-start.1 = ((bf16[16,96,2048]{2,1,0:T(8,128)(2,1)}), bf16[16,96,2048]{2,1,0:T(8,128)(2,1)}, u32[]{:S(2)}, u32[]{:S(2)}) async-start(bf16[16,96,2048]{2,1,0:T(8,128)(2,1)} %convolution_convert_fusion), calls=%async_computation.1 | async-start | bytes 12582912 | tf_op jit(solution)/shard_map/all_to_all | solution.py:50
where the time goes:
time: 329 us
  blocking collectives  148 us (45%)
  waiting for transfers between devices  146 us (44%)
  matrix products  17.5 us (5%)
  starting transfers between devices  7.18 us (2%)
  other arithmetic  6.2 us (2%)
  local copies, waits for them, and re-layouts  3.65 us (1%)
    all_to_all x1, blocking collectives, local(): lax.all_to_all(outgoing, 'expert', split_axis=0, concat_axis=0, tiled=True)  148 us
    all_to_all x1, waiting for transfers between devices, local(): lax.all_to_all(expert_rows(received, wgate, wup, wdown), 'expert', split_...  139 us
    dot_general x1, matrix products, expert_rows(): jnp.einsum('sch,hd->scd', hidden, wdown, preferred_element_type=jnp.float32)  12.3 us
    ppermute x1, waiting for transfers between devices, shifted(): return lax.ppermute(value, axis, pairs)  7.73 us
  transfers between devices with their start and end apart: 2, of which 2 were waited for; matrix products, arithmetic and copies ran while one was open for 0% of the time, Pallas kernels for 0%

commit v1 on v0

v1 whole, which is shorter than its diff:
```python
import functools

import jax
import jax.numpy as jnp
from jax import lax
from jax.experimental import pallas as pl
from jax.experimental.pallas import tpu as pltpu
from jax.sharding import PartitionSpec as P

NEXP = 4
CAP = 96
SHIFT_PARTS = 4
MESH = pl.DeviceIdType.MESH
F32 = jnp.float32
BF16 = jnp.bfloat16


def far_order(y, k):
    low = y < 2
    yy = jnp.where(low, y, 3 - y)
    d = 3 - k
    d = jnp.where(d <= yy, d - 1, d)
    return jnp.where(low, d, 3 - d)


def kernel(
    acts, routes, gates, gain, gate_w, up_w, down_w, out,
    inc, packs, rows, wg, wu, wd, normed, hidden, own_part, mate_part, got_part,
    summed, back, place_t, place, gate_of,
    shift_s, shift_r, w_s, w_r, w_l, y_s, y_r, rel_s, rel_r, part_s, part_r, ret_s, ret_r,
):
    tok, dim = inc.shape
    width = gate_w.shape[1]
    n_sec = lax.axis_size("section")
    s = lax.axis_index("section")
    e = lax.axis_index("expert")
    core = lax.rem(s, 2)
    x = lax.rem(e, 4)
    y = e // 4
    flip = x + 1 - 2 * lax.rem(x, 2)
    cross = 3 - x
    wx = jnp.where(core == 0, flip, cross)
    tx = jnp.where(core == 0, cross, flip)
    nxt = (lax.rem(s + 1, n_sec), e)
    prv = (lax.rem(s + n_sec - 1, n_sec), e)
    wmate = (s, y * 4 + wx)
    tmate = (s, y * 4 + tx)

    def at_row(r):
        return (s, r * 4 + x)

    barrier = pltpu.get_barrier_semaphore()
    for peer in (nxt, prv, wmate, tmate):
        pl.semaphore_signal(barrier, inc=1, device_id=peer, device_id_type=MESH)
    for i in range(1, 4):
        pl.semaphore_signal(barrier, inc=1, device_id=at_row(lax.rem(y + i, 4)), device_id_type=MESH)

    local = [
        pltpu.make_async_copy(gate_w, wg.at[0], w_l.at[0]),
        pltpu.make_async_copy(up_w, wu.at[0], w_l.at[1]),
        pltpu.make_async_copy(down_w, wd.at[pl.ds(0, width)], w_l.at[2]),
    ]
    for copy in local:
        copy.start()
    pl.semaphore_wait(barrier, 7)

    part = dim // SHIFT_PARTS
    shifts = [
        pltpu.make_async_remote_copy(
            acts.at[:, pl.ds(i * part, part)], inc.at[:, pl.ds(i * part, part)],
            shift_s.at[i], shift_r.at[i], device_id=nxt, device_id_type=MESH)
        for i in range(SHIFT_PARTS)
    ]
    for copy in shifts:
        copy.start()
    weights = [
        pltpu.make_async_remote_copy(src, dst, w_s.at[i], w_r.at[i], device_id=wmate, device_id_type=MESH)
        for i, (src, dst) in enumerate(
            ((gate_w, wg.at[1]), (up_w, wu.at[1]), (down_w, wd.at[pl.ds(width, width)])))
    ]
    for copy in weights:
        copy.start()

    lane = lax.broadcasted_iota(jnp.int32, (tok, tok), 1)
    sub = lax.broadcasted_iota(jnp.int32, (tok, tok), 0)
    first, second = routes[:, 0:1] == lane, routes[:, 1:2] == lane
    member = (first | second).astype(F32)
    gate_of[...] = jnp.where(first, gates[:, 0:1], 0.0) + jnp.where(second, gates[:, 1:2], 0.0)
    tri = (lane <= sub).astype(BF16)
    rank = jnp.dot(tri, member.astype(BF16), preferred_element_type=F32) - 1.0
    slot = lane.astype(F32)
    for g in range(NEXP):
        hot = jnp.where(rank[:, g:g + 1] == slot, member[:, g:g + 1], 0.0)
        place_t[g] = hot.astype(BF16)
        place[g] = hot.T.astype(BF16)

    def packed(g, cols):
        return jnp.dot(place[g][:CAP], inc[:, cols], preferred_element_type=F32).astype(BF16)

    for i in range(SHIFT_PARTS):
        shifts[i].wait_recv()
        cols = pl.ds(i * part, part)
        for k in range(3):
            packs[k, :, cols] = packed(far_order(y, k), cols)
        rows[y, 0, :, cols] = packed(y, cols)

    def dispatch(k):
        return pltpu.make_async_remote_copy(
            packs.at[k], rows.at[y, 0], y_s.at[k], y_r.at[y],
            device_id=at_row(far_order(y, k)), device_id_type=MESH)

    for k in range(3):
        dispatch(k).start()

    def arrival(src):
        return pltpu.make_async_remote_copy(
            packs.at[0], rows.at[src, 0], y_s.at[0], y_r.at[src],
            device_id=at_row(src), device_id_type=MESH)

    def relay(src):
        return pltpu.make_async_remote_copy(
            rows.at[src, 0], rows.at[src, 1], rel_s.at[src], rel_r.at[src],
            device_id=tmate, device_id_type=MESH)

    def norm(src, which):
        xf = rows[src, which].astype(F32)
        scale = lax.rsqrt(jnp.mean(xf * xf, axis=1, keepdims=True) + 1e-06)
        normed[src, pl.ds(which * CAP, CAP), :] = (xf * scale * gain[...]).astype(BF16)

    def activate(src, half):
        xn = normed[src]
        gpart = jnp.dot(xn, wg[half], preferred_element_type=F32)
        upart = jnp.dot(xn, wu[half], preferred_element_type=F32)
        hidden[src, :, pl.ds(half * width, width)] = (jax.nn.silu(gpart) * upart).astype(BF16)

    for copy in local:
        copy.wait()

    @pl.loop(0, 5)
    def _(b):
        @pl.when(b < 4)
        def _():
            src = lax.rem(y + b, 4)

            @pl.when(b > 0)
            def _():
                arrival(src).wait_recv()

            relay(src).start()
            norm(src, 0)

        @pl.when(b > 0)
        def _():
            src = lax.rem(y + b + 3, 4)
            relay(src).wait_recv()
            norm(src, 1)
            activate(src, 0)

    for copy in weights:
        copy.wait_recv()

    def partial(src):
        return pltpu.make_async_remote_copy(
            mate_part.at[src], got_part.at[src], part_s.at[src], part_r.at[src],
            device_id=tmate, device_id_type=MESH)

    def giveback(src):
        return pltpu.make_async_remote_copy(
            summed.at[src], back.at[y], ret_s.at[src], ret_r.at[y],
            device_id=at_row(src), device_id_type=MESH)

    tile = dim // 4

    @pl.loop(0, 5)
    def _(b):
        @pl.when(b < 4)
        def _():
            src = lax.rem(y + b + 1, 4)
            activate(src, 1)
            hid = hidden[src]
            for t in range(4):
                cols = pl.ds(t * tile, tile)
                value = jnp.dot(hid, wd[:, cols], preferred_element_type=F32)
                own_part[src, :, cols] = value[:CAP]
                mate_part[src, :, cols] = value[CAP:].astype(BF16)
            partial(src).start()

        @pl.when(b > 0)
        def _():
            src = lax.rem(y + b, 4)
            partial(src).wait_recv()
            total = (own_part[src] + got_part[src].astype(F32)).astype(BF16)

            @pl.when(b < 4)
            def _():
                summed[src] = total
                giveback(src).start()

            @pl.when(b == 4)
            def _():
                back[y] = total

    for i in range(1, 4):
        g = lax.rem(y + i, 4)
        pltpu.make_async_remote_copy(
            summed.at[0], back.at[g], ret_s.at[0], ret_r.at[g],
            device_id=at_row(g), device_id_type=MESH).wait_recv()

    for t in range(4):
        cols = pl.ds(t * tile, tile)
        total = inc[:, cols].astype(F32)
        for g in range(NEXP):
            total = total + gate_of[:, g:g + 1] * jnp.dot(
                place_t[g][:, :CAP], back[g, :, cols], preferred_element_type=F32)
        out[:, cols] = total.astype(BF16)

    for copy in shifts:
        copy.wait_send()
    for copy in weights:
        copy.wait_send()
    for k in range(3):
        dispatch(k).wait_send()
    for i in range(4):
        relay(i).wait_send()
        partial(i).wait_send()
    for i in range(1, 4):
        giveback(lax.rem(y + i, 4)).wait_send()


def local(acts, routes, gates, norm_gain, gate_w, up_w, down_w):
    tok, dim = acts.shape[1:]
    width = gate_w.shape[2]
    hbm = pl.BlockSpec(memory_space=pl.ANY)
    vmem = pl.BlockSpec(memory_space=pltpu.VMEM)
    dma = pltpu.SemaphoreType.DMA
    both = 2 * CAP
    result = pl.pallas_call(
        kernel,
        name="relay_experts",
        out_shape=jax.ShapeDtypeStruct((tok, dim), BF16),
        in_specs=[hbm, vmem, vmem, vmem, hbm, hbm, hbm],
        out_specs=vmem,
        scratch_shapes=[
            pltpu.VMEM((tok, dim), BF16),
            pltpu.VMEM((3, CAP, dim), BF16),
            pltpu.VMEM((4, 2, CAP, dim), BF16),
            pltpu.VMEM((2, dim, width), BF16),
            pltpu.VMEM((2, dim, width), BF16),
            pltpu.VMEM((2 * width, dim), BF16),
            pltpu.VMEM((4, both, dim), BF16),
            pltpu.VMEM((4, both, 2 * width), BF16),
            pltpu.VMEM((4, CAP, dim), F32),
            pltpu.VMEM((4, CAP, dim), BF16),
            pltpu.VMEM((4, CAP, dim), BF16),
            pltpu.VMEM((4, CAP, dim), BF16),
            pltpu.VMEM((4, CAP, dim), BF16),
            pltpu.VMEM((4, tok, tok), BF16),
            pltpu.VMEM((4, tok, tok), BF16),
            pltpu.VMEM((tok, tok), F32),
            dma((SHIFT_PARTS,)), dma((SHIFT_PARTS,)),
            dma((3,)), dma((3,)), dma((3,)),
            dma((3,)), dma((4,)),
            dma((4,)), dma((4,)),
            dma((4,)), dma((4,)),
            dma((4,)), dma((4,)),
        ],
        compiler_params=pltpu.CompilerParams(
            collective_id=0, has_side_effects=True, vmem_limit_bytes=56 * 1024 * 1024),
    )(acts[0], routes[0], gates[0], norm_gain, gate_w[0], up_w[0], down_w[0])
    return result.reshape(1, tok, dim)


def solution(mesh):
    in_specs = (
        P("section", "expert", None),
        P("section", "expert", None),
        P("section", "expert", None),
        P("section", None),
        P("section", None, "expert"),
        P("section", None, "expert"),
        P("section", "expert", None),
    )
    out_specs = P("section", "expert", None)
    return jax.shard_map(local, mesh=mesh, in_specs=in_specs, out_specs=out_specs, check_vma=False)
```

time: 329 us -> 118 us (0.36)
  the two profiles are of different devices: /device:TPU:208 before, /device:TPU:25 now
where the time goes in v1:
time: 118 us
  Pallas kernels  113 us (96%)
  local copies, waits for them, and re-layouts  4.71 us (4%)
    pallas_call x1, Pallas kernels, local(): pl.pallas_call(kernel, name='relay_experts', out_shape=jax.ShapeDtypeStru...  113 us
    unnamed x7, local copies, waits for them, and re-layouts  4.71 us

profile of v1, /device:TPU:25, one launch (start us, length us, event | category | flops | bytes accessed | tf_op | source)
XLA Modules:
  0.0 117.6 jit_solution(4671882594517613250)
XLA Ops:
  0.0 0.0 copy-start
  0.0 0.7 copy-done
  0.7 0.7 copy.8
  1.4 0.0 copy-start.1
  1.4 0.7 copy-done.1
  2.1 0.7 copy.9
  2.8 112.8 %relay_experts.1 = bf16[128,2048]{1,0:T(8,128)(2,1)} custom-call(bf16[128,2048]{1,0:T(8,128)(2,1)} %bitcast.11, s32[128,2]{1,0:T(8,128)} %bitcast.12, f32[128,2]{1,0:T(8,128)} %bitcast.13, f32[1,2048]{1,0:T(1,128)} %gain.1, bf16[2048,256]{1,0:T(8,128)(2,1)} %bitcast.8, bf16[2048,256]{1,0:T(8,128)(2,1)} %bitcast.9, bf16[256,2048]{1,0:T(8,128)(2,1)} %bitcast.10), custom_call_target="tpu_custom_call" | custom-call | tf_op jit(solution)/shard_map/relay_experts/pallas_call | solution.py:237
  115.7 1.9 %copy.11 = bf16[1,128,2048]{2,1,0:T(8,128)(2,1)} copy(bf16[1,128,2048]{2,1,0:T(8,128)(2,1)} %bitcast.7) | data formatting | bytes 1048576
Async XLA Ops:
  0.0 0.7 copy-start
  1.4 0.7 copy-start.1

commit v2 on v1

v2 whole, which is shorter than its diff:
```python
import functools

import jax
import jax.numpy as jnp
from jax import lax
from jax.experimental import pallas as pl
from jax.experimental.pallas import tpu as pltpu
from jax.sharding import PartitionSpec as P

NEXP = 4
CAP = 96
SHIFT_PARTS = 4
EARLY = 2
MESH = pl.DeviceIdType.MESH
F32 = jnp.float32
BF16 = jnp.bfloat16


def far_order(y, k):
    low = y < 2
    yy = jnp.where(low, y, 3 - y)
    d = 3 - k
    d = jnp.where(d <= yy, d - 1, d)
    return jnp.where(low, d, 3 - d)


def kernel(
    acts, routes, gates, gain, gate_w, up_w, down_w, out,
    inc, hop, packs, rows, wg, wu, wd, normed, hidden, own_part, mate_part, got_part,
    summed, back, place_t, place, gate_of,
    shift_s, shift_r, hop_s, hop_r, w_s, w_r, w_l, y_s, y_r, rel_s, rel_r, part_s, part_r, ret_s, ret_r,
):
    tok, dim = inc.shape
    width = gate_w.shape[1]
    n_sec = lax.axis_size("section")
    half = n_sec // 2
    s = lax.axis_index("section")
    e = lax.axis_index("expert")
    core = lax.rem(s, 2)
    x = lax.rem(e, 4)
    y = e // 4
    flip = x + 1 - 2 * lax.rem(x, 2)
    cross = 3 - x
    wx = jnp.where(core == 0, flip, cross)
    tx = jnp.where(core == 0, cross, flip)
    nxt = (lax.rem(s + 1, n_sec), e)
    prv = (lax.rem(s + n_sec - 1, n_sec), e)
    wmate = (s, y * 4 + wx)
    tmate = (s, y * 4 + tx)
    leaves = lax.rem(s, half) == half - 1
    enters = lax.rem(s, half) == 0
    ring = (s // half) * 4 + y

    def around(steps, last):
        to = lax.rem(ring + 8 + steps, 8)
        return ((to // 4) * half + last * (half - 1), lax.rem(to, 4) * 4 + x)

    def at_row(r):
        return (s, r * 4 + x)

    def greet(peer):
        pl.semaphore_signal(barrier, inc=1, device_id=peer, device_id_type=MESH)

    barrier = pltpu.get_barrier_semaphore()
    greet(wmate)
    greet(tmate)
    for i in range(1, 4):
        greet(at_row(lax.rem(y + i, 4)))

    @pl.when(enters)
    def _():
        for last in range(2):
            greet(around(2, last))
            greet(around(-2, last))

    @pl.when(jnp.logical_not(enters))
    def _():
        greet(prv)

    local = [
        pltpu.make_async_copy(gate_w, wg.at[0], w_l.at[0]),
        pltpu.make_async_copy(up_w, wu.at[0], w_l.at[1]),
        pltpu.make_async_copy(down_w, wd.at[pl.ds(0, width)], w_l.at[2]),
    ]
    for copy in local:
        copy.start()
    pl.semaphore_wait(barrier, 6 + jnp.where(leaves, 1, 0) + jnp.where(enters, 2, 0))

    part = dim // SHIFT_PARTS
    columns = [pl.ds(i * part, part) for i in range(SHIFT_PARTS)]

    def shift(i, peer):
        return pltpu.make_async_remote_copy(
            acts.at[:, columns[i]], inc.at[:, columns[i]],
            shift_s.at[i], shift_r.at[i], device_id=peer, device_id_type=MESH)

    def first_leg(i):
        return pltpu.make_async_remote_copy(
            acts.at[:, columns[i]], hop.at[:, columns[i]], shift_s.at[i], hop_r.at[i],
            device_id=around(2 if i % 2 == 0 else -2, 0), device_id_type=MESH)

    def second_leg(i):
        return pltpu.make_async_remote_copy(
            hop.at[:, columns[i]], inc.at[:, columns[i]], hop_s.at[i], shift_r.at[i],
            device_id=around(2 if i % 2 == 0 else -2, 0), device_id_type=MESH)

    @pl.when(leaves)
    def _():
        for i in range(SHIFT_PARTS):
            first_leg(i).start()

    @pl.when(jnp.logical_not(leaves))
    def _():
        for i in range(SHIFT_PARTS):
            shift(i, nxt).start()

    weights = [
        pltpu.make_async_remote_copy(src, dst, w_s.at[i], w_r.at[i], device_id=wmate, device_id_type=MESH)
        for i, (src, dst) in enumerate(
            ((gate_w, wg.at[1]), (up_w, wu.at[1]), (down_w, wd.at[pl.ds(width, width)])))
    ]
    for copy in weights:
        copy.start()

    lane = lax.broadcasted_iota(jnp.int32, (tok, tok), 1)
    sub = lax.broadcasted_iota(jnp.int32, (tok, tok), 0)
    first, second = routes[0:1, :] == sub, routes[1:2, :] == sub
    member = (first | second).astype(F32)
    gate_of[...] = (jnp.where(first, gates[0:1, :], 0.0) + jnp.where(second, gates[1:2, :], 0.0)).T
    rank = jnp.dot(member.astype(BF16), (sub <= lane).astype(BF16), preferred_element_type=F32) - 1.0
    slot = sub.astype(F32)
    for g in range(NEXP):
        hot = jnp.where(rank[g:g + 1, :] == slot, member[g:g + 1, :], 0.0)
        place[g] = hot.astype(BF16)
        place_t[g] = hot.T.astype(BF16)

    @pl.when(enters)
    def _():
        for i in range(SHIFT_PARTS):
            first_leg(i).wait_recv()
            second_leg(i).start()

    def packed(g, cols):
        return jnp.dot(place[g][:CAP], inc[:, cols], preferred_element_type=F32).astype(BF16)

    for i in range(SHIFT_PARTS):
        shift(i, nxt).wait_recv()
        cols = columns[i]
        for k in range(3):
            packs[k, :, cols] = packed(far_order(y, k), cols)
        rows[0, y, :, cols] = packed(y, cols)

    def dispatch(k):
        return pltpu.make_async_remote_copy(
            packs.at[k], rows.at[0, y], y_s.at[k], y_r.at[y],
            device_id=at_row(far_order(y, k)), device_id_type=MESH)

    for k in range(3):
        dispatch(k).start()

    def arrival(src):
        return pltpu.make_async_remote_copy(
            packs.at[0], rows.at[0, src], y_s.at[0], y_r.at[src],
            device_id=at_row(src), device_id_type=MESH)

    def relay(src):
        return pltpu.make_async_remote_copy(
            rows.at[0, src], rows.at[1, src], rel_s.at[src], rel_r.at[src],
            device_id=tmate, device_id_type=MESH)

    def block(b):
        return jnp.where(b == 3, y, far_order(y, jnp.minimum(b, 2)))

    def norm(which, src):
        xf = rows[which, src].astype(F32)
        scale = lax.rsqrt(jnp.mean(xf * xf, axis=1, keepdims=True) + 1e-06)
        return (xf * scale * gain[...]).astype(BF16)

    def activate(xn, part):
        gpart = jnp.dot(xn, wg[part], preferred_element_type=F32)
        upart = jnp.dot(xn, wu[part], preferred_element_type=F32)
        return (jax.nn.silu(gpart) * upart).astype(BF16)

    normed[y] = norm(0, y)

    @pl.loop(0, 3)
    def _(b):
        src = block(b)
        arrival(src).wait_recv()

        @pl.when(b < EARLY)
        def _():
            relay(src).start()

        normed[src] = norm(0, src)

    for b in range(3, EARLY):
        relay(block(b)).start()

    for copy in local:
        copy.wait()

    def own_rows(part):
        for pair in range(2):
            xn = normed[pl.ds(2 * pair, 2)].reshape(2 * CAP, dim)
            hidden[pl.ds(2 * pair, 2), :, pl.ds(part * width, width)] = activate(xn, part).reshape(2, CAP, width)

    own_rows(0)
    weights[0].wait_recv()
    weights[1].wait_recv()
    own_rows(1)
    weights[2].wait_recv()

    def partial(src):
        return pltpu.make_async_remote_copy(
            mate_part.at[src], got_part.at[src], part_s.at[src], part_r.at[src],
            device_id=tmate, device_id_type=MESH)

    def giveback(src):
        return pltpu.make_async_remote_copy(
            summed.at[src], back.at[y], ret_s.at[src], ret_r.at[y],
            device_id=at_row(src), device_id_type=MESH)

    tile = dim // 4

    @pl.loop(0, 5)
    def _(b):
        @pl.when(b < 4)
        def _():
            src = block(b)
            relay(src).wait_recv()
            xn = norm(1, src)
            hid = jnp.concatenate([activate(xn, 0), activate(xn, 1)], axis=1)
            for t in range(4):
                cols = pl.ds(t * tile, tile)
                mate_part[src, :, cols] = jnp.dot(hid, wd[:, cols], preferred_element_type=F32).astype(BF16)
            partial(src).start()

            @pl.when(b + EARLY < 4)
            def _():
                relay(block(b + EARLY)).start()

            hid = hidden[src]
            for t in range(4):
                cols = pl.ds(t * tile, tile)
                own_part[src, :, cols] = jnp.dot(hid, wd[:, cols], preferred_element_type=F32)

        @pl.when(b > 0)
        def _():
            src = block(b - 1)
            partial(src).wait_recv()
            total = (own_part[src] + got_part[src].astype(F32)).astype(BF16)

            @pl.when(b < 4)
            def _():
                summed[src] = total
                giveback(src).start()

            @pl.when(b == 4)
            def _():
                back[y] = total

    for i in range(1, 4):
        g = lax.rem(y + i, 4)
        pltpu.make_async_remote_copy(
            summed.at[0], back.at[g], ret_s.at[0], ret_r.at[g],
            device_id=at_row(g), device_id_type=MESH).wait_recv()

    for t in range(4):
        cols = pl.ds(t * tile, tile)
        total = inc[:, cols].astype(F32)
        for g in range(NEXP):
            total = total + gate_of[:, g:g + 1] * jnp.dot(
                place_t[g][:, :CAP], back[g, :, cols], preferred_element_type=F32)
        out[:, cols] = total.astype(BF16)

    for i in range(SHIFT_PARTS):
        shift(i, nxt).wait_send()

    @pl.when(enters)
    def _():
        for i in range(SHIFT_PARTS):
            second_leg(i).wait_send()

    for copy in weights:
        copy.wait_send()
    for k in range(3):
        dispatch(k).wait_send()
    for i in range(4):
        relay(i).wait_send()
        partial(i).wait_send()
    for i in range(1, 4):
        giveback(lax.rem(y + i, 4)).wait_send()


def local(acts, routes, gates, norm_gain, gate_w, up_w, down_w):
    tok, dim = acts.shape[1:]
    width = gate_w.shape[2]
    hbm = pl.BlockSpec(memory_space=pl.ANY)
    vmem = pl.BlockSpec(memory_space=pltpu.VMEM)
    dma = pltpu.SemaphoreType.DMA
    result = pl.pallas_call(
        kernel,
        name="relay_experts",
        out_shape=jax.ShapeDtypeStruct((tok, dim), BF16),
        in_specs=[hbm, vmem, vmem, vmem, hbm, hbm, hbm],
        out_specs=vmem,
        scratch_shapes=[
            pltpu.VMEM((tok, dim), BF16),
            pltpu.VMEM((tok, dim), BF16),
            pltpu.VMEM((3, CAP, dim), BF16),
            pltpu.VMEM((2, 4, CAP, dim), BF16),
            pltpu.VMEM((2, dim, width), BF16),
            pltpu.VMEM((2, dim, width), BF16),
            pltpu.VMEM((2 * width, dim), BF16),
            pltpu.VMEM((4, CAP, dim), BF16),
            pltpu.VMEM((4, CAP, 2 * width), BF16),
            pltpu.VMEM((4, CAP, dim), F32),
            pltpu.VMEM((4, CAP, dim), BF16),
            pltpu.VMEM((4, CAP, dim), BF16),
            pltpu.VMEM((4, CAP, dim), BF16),
            pltpu.VMEM((4, CAP, dim), BF16),
            pltpu.VMEM((4, tok, tok), BF16),
            pltpu.VMEM((4, tok, tok), BF16),
            pltpu.VMEM((tok, tok), F32),
            dma((SHIFT_PARTS,)), dma((SHIFT_PARTS,)),
            dma((SHIFT_PARTS,)), dma((SHIFT_PARTS,)),
            dma((3,)), dma((3,)), dma((3,)),
            dma((3,)), dma((4,)),
            dma((4,)), dma((4,)),
            dma((4,)), dma((4,)),
            dma((4,)), dma((4,)),
        ],
        compiler_params=pltpu.CompilerParams(
            collective_id=0, has_side_effects=True, vmem_limit_bytes=56 * 1024 * 1024),
    )(acts[0], routes[0].T, gates[0].T, norm_gain, gate_w[0], up_w[0], down_w[0])
    return result.reshape(1, tok, dim)


def solution(mesh):
    in_specs = (
        P("section", "expert", None),
        P("section", "expert", None),
        P("section", "expert", None),
        P("section", None),
        P("section", None, "expert"),
        P("section", None, "expert"),
        P("section", "expert", None),
    )
    out_specs = P("section", "expert", None)
    return jax.shard_map(local, mesh=mesh, in_specs=in_specs, out_specs=out_specs, check_vma=False)
```

time: 118 us -> 97.4 us (0.83)
  the two profiles are of different devices: /device:TPU:25 before, /device:TPU:10 now
where the time goes in v2:
time: 97.4 us; the launch traced here: 97.2 us
  Pallas kernels  95.3 us (98%)
  local copies, waits for them, and re-layouts  1.88 us (2%)
    pallas_call x1, Pallas kernels, local(): pl.pallas_call(kernel, name='relay_experts', out_shape=jax.ShapeDtypeStru...  95.3 us

profile of v2, /device:TPU:10, one launch (start us, length us, event | category | flops | bytes accessed | tf_op | source)
XLA Modules:
  0.0 97.2 jit_solution(5198372724569236101)
XLA Ops:
  0.0 95.3 %relay_experts.1 = bf16[128,2048]{1,0:T(8,128)(2,1)} custom-call(bf16[128,2048]{1,0:T(8,128)(2,1)} %bitcast.15, s32[2,128]{1,0:T(2,128)} %bitcast.16, f32[2,128]{1,0:T(2,128)} %bitcast.17, f32[1,2048]{1,0:T(1,128)} %gain.1, bf16[2048,256]{1,0:T(8,128)(2,1)} %bitcast.12, bf16[2048,256]{1,0:T(8,128)(2,1)} %bitcast.13, bf16[256,2048]{1,0:T(8,128)(2,1)} %bitcast.14), custom_call_target="tpu_custom_call" | custom-call | tf_op jit(solution)/shard_map/relay_experts/pallas_call | solution.py:302
  95.4 1.9 %copy.9 = bf16[1,128,2048]{2,1,0:T(8,128)(2,1)} copy(bf16[1,128,2048]{2,1,0:T(8,128)(2,1)} %bitcast.11) | data formatting | bytes 1048576

commit v3 on v2

--- a/solution.py
+++ b/solution.py
@@ -10,7 +10,12 @@
 NEXP = 4
 CAP = 96
 SHIFT_PARTS = 4
-EARLY = 2
+EARLY = 1
+SOON = 2
+PARTS = 2
+PAIR = 1
+LAG = 2
+JOIN = 1
 MESH = pl.DeviceIdType.MESH
 F32 = jnp.float32
 BF16 = jnp.bfloat16
@@ -26,9 +31,10 @@
 
 def kernel(
     acts, routes, gates, gain, gate_w, up_w, down_w, out,
-    inc, hop, packs, rows, wg, wu, wd, normed, hidden, own_part, mate_part, got_part,
-    summed, back, place_t, place, gate_of,
+    inc, hop, packs, far_rows, onward, rows, wg, wu, wd, normed, mate_normed, hidden, mate_hidden, own_part, mate_part, got_part,
+    summed, back, via, joined, given_in, total, place_t, place, gate_of, far_routes, far_gates, far_place, far_pick, far_gate_of,
     shift_s, shift_r, hop_s, hop_r, w_s, w_r, w_l, y_s, y_r, rel_s, rel_r, part_s, part_r, ret_s, ret_r,
+    via_r, join_s, join_r, meta_s, meta_r, far_s, far_r, on_s,
 ):
     tok, dim = inc.shape
     width = gate_w.shape[1]
@@ -114,25 +120,53 @@
         for i in range(SHIFT_PARTS):
             shift(i, nxt).start()
 
-    weights = [
-        pltpu.make_async_remote_copy(src, dst, w_s.at[i], w_r.at[i], device_id=wmate, device_id_type=MESH)
-        for i, (src, dst) in enumerate(
-            ((gate_w, wg.at[1]), (up_w, wu.at[1]), (down_w, wd.at[pl.ds(width, width)])))
+    tile = dim // PARTS
+    narrow = [
+        pltpu.make_async_remote_copy(src, dst.at[1], w_s.at[i], w_r.at[i], device_id=wmate, device_id_type=MESH)
+        for i, (src, dst) in enumerate(((gate_w, wg), (up_w, wu)))
     ]
-    for copy in weights:
+
+    def columns_of(h):
+        return pl.ds(pl.multiple_of(h * tile, tile), tile)
+
+    def wide(h):
+        return pltpu.make_async_remote_copy(
+            down_w.at[:, columns_of(h)], wd.at[pl.ds(width, width), columns_of(h)], w_s.at[2 + h], w_r.at[2 + h],
+            device_id=wmate, device_id_type=MESH)
+
+    for copy in narrow:
+        copy.start()
+    for h in range(PARTS):
+        wide(h).start()
+
+    inner = (y == 1) | (y == 2)
+    mate = y + 1 - 2 * lax.rem(y, 2)
+    across = jnp.where(y < 2, 2, 1)
+    mine = jnp.where(inner, 1, 0)
+    meta = [
+        pltpu.make_async_remote_copy(
+            src, dst.at[mine], meta_s.at[i], meta_r.at[mine, i], device_id=at_row(across), device_id_type=MESH)
+        for i, (src, dst) in enumerate(((routes, far_routes), (gates, far_gates)))
+    ]
+    for copy in meta:
         copy.start()
 
     lane = lax.broadcasted_iota(jnp.int32, (tok, tok), 1)
     sub = lax.broadcasted_iota(jnp.int32, (tok, tok), 0)
-    first, second = routes[0:1, :] == sub, routes[1:2, :] == sub
-    member = (first | second).astype(F32)
-    gate_of[...] = (jnp.where(first, gates[0:1, :], 0.0) + jnp.where(second, gates[1:2, :], 0.0)).T
-    rank = jnp.dot(member.astype(BF16), (sub <= lane).astype(BF16), preferred_element_type=F32) - 1.0
     slot = sub.astype(F32)
+
+    def table(ids, weights):
+        first, second = ids[0:1, :] == sub, ids[1:2, :] == sub
+        member = (first | second).astype(F32)
+        gate = jnp.where(first, weights[0:1, :], 0.0) + jnp.where(second, weights[1:2, :], 0.0)
+        rank = jnp.dot(member.astype(BF16), (sub <= lane).astype(BF16), preferred_element_type=F32) - 1.0
+        hots = [jnp.where(rank[g:g + 1, :] == slot, member[g:g + 1, :], 0.0) for g in range(NEXP)]
+        return gate.T, hots
+
+    gate_of[...], hots = table(routes[...], gates[...])
     for g in range(NEXP):
-        hot = jnp.where(rank[g:g + 1, :] == slot, member[g:g + 1, :], 0.0)
-        place[g] = hot.astype(BF16)
-        place_t[g] = hot.T.astype(BF16)
+        place[g] = hots[g].astype(BF16)
+        place_t[g] = hots[g].T.astype(BF16)
 
     @pl.when(enters)
     def _():
@@ -143,25 +177,53 @@
     def packed(g, cols):
         return jnp.dot(place[g][:CAP], inc[:, cols], preferred_element_type=F32).astype(BF16)
 
+    def crossing(i, to):
+        return pltpu.make_async_remote_copy(
+            inc.at[:, columns[i]], far_rows.at[to, :, columns[i]], far_s.at[i], far_r.at[to, i],
+            device_id=at_row(across), device_id_type=MESH)
+
     for i in range(SHIFT_PARTS):
         shift(i, nxt).wait_recv()
         cols = columns[i]
-        for k in range(3):
-            packs[k, :, cols] = packed(far_order(y, k), cols)
+        crossing(i, mine).start()
+        packs[:, cols] = packed(mate, cols)
         rows[0, y, :, cols] = packed(y, cols)
 
-    def dispatch(k):
-        return pltpu.make_async_remote_copy(
-            packs.at[k], rows.at[0, y], y_s.at[k], y_r.at[y],
-            device_id=at_row(far_order(y, k)), device_id_type=MESH)
-
-    for k in range(3):
-        dispatch(k).start()
+    dispatch = pltpu.make_async_remote_copy(
+        packs, rows.at[0, y], y_s.at[0], y_r.at[y], device_id=at_row(mate), device_id_type=MESH)
+    dispatch.start()
+
+    def passing(b, i):
+        src = far_order(y, b)
+        return pltpu.make_async_remote_copy(
+            onward.at[b, :, columns[i]], rows.at[0, src, :, columns[i]], on_s.at[b, i], y_r.at[src],
+            device_id=at_row(mate), device_id_type=MESH)
+
+    @pl.when(inner)
+    def _():
+        for i in range(2):
+            for j, (src, dst) in enumerate(((routes, far_routes), (gates, far_gates))):
+                pltpu.make_async_remote_copy(
+                    src, dst.at[i], meta_s.at[j], meta_r.at[i, j], device_id=at_row(across),
+                    device_id_type=MESH).wait_recv()
+            far_gate_of[i], far_hots = table(far_routes[i], far_gates[i])
+            for g in range(NEXP):
+                far_pick[i, g] = far_hots[g].astype(BF16)
+                far_place[i, g] = far_hots[g].T.astype(BF16)
+        for i in range(SHIFT_PARTS):
+            for b in range(2):
+                crossing(i, b).wait_recv()
+                value = far_rows[b, :, columns[i]]
+                onward[b, :, columns[i]] = jnp.dot(
+                    far_pick[b, mate][:CAP], value, preferred_element_type=F32).astype(BF16)
+                passing(b, i).start()
+                rows[0, far_order(y, b), :, columns[i]] = jnp.dot(
+                    far_pick[b, y][:CAP], value, preferred_element_type=F32).astype(BF16)
 
     def arrival(src):
         return pltpu.make_async_remote_copy(
-            packs.at[0], rows.at[0, src], y_s.at[0], y_r.at[src],
-            device_id=at_row(src), device_id_type=MESH)
+            packs, rows.at[0, src], y_s.at[0], y_r.at[src],
+            device_id=at_row(mate), device_id_type=MESH)
 
     def relay(src):
         return pltpu.make_async_remote_copy(
@@ -181,21 +243,25 @@
         upart = jnp.dot(xn, wu[part], preferred_element_type=F32)
         return (jax.nn.silu(gpart) * upart).astype(BF16)
 
+    @pl.when(enters)
+    def _():
+        relay(y).start()
+
     normed[y] = norm(0, y)
 
     @pl.loop(0, 3)
     def _(b):
         src = block(b)
-        arrival(src).wait_recv()
-
-        @pl.when(b < EARLY)
+
+        @pl.when((b == 2) | jnp.logical_not(inner))
+        def _():
+            arrival(src).wait_recv()
+
+        @pl.when((b < EARLY) | enters)
         def _():
             relay(src).start()
 
         normed[src] = norm(0, src)
-
-    for b in range(3, EARLY):
-        relay(block(b)).start()
 
     for copy in local:
         copy.wait()
@@ -206,73 +272,139 @@
             hidden[pl.ds(2 * pair, 2), :, pl.ds(part * width, width)] = activate(xn, part).reshape(2, CAP, width)
 
     own_rows(0)
-    weights[0].wait_recv()
-    weights[1].wait_recv()
-    own_rows(1)
-    weights[2].wait_recv()
-
-    def partial(src):
-        return pltpu.make_async_remote_copy(
-            mate_part.at[src], got_part.at[src], part_s.at[src], part_r.at[src],
+    relay(block(0)).wait_recv()
+    mate_normed[...] = norm(1, block(0))
+    mate_hidden[block(0), :, pl.ds(0, width)] = activate(mate_normed[...], 0)
+    narrow[0].wait_recv()
+
+    @pl.when(jnp.logical_not(enters))
+    def _():
+        for b in range(EARLY, SOON):
+            relay(block(b)).start()
+
+    narrow[1].wait_recv()
+
+    def partial(src, h):
+        return pltpu.make_async_remote_copy(
+            mate_part.at[src, :, columns_of(h)], got_part.at[src, :, columns_of(h)], part_s.at[src, h], part_r.at[src, h],
             device_id=tmate, device_id_type=MESH)
 
-    def giveback(src):
-        return pltpu.make_async_remote_copy(
-            summed.at[src], back.at[y], ret_s.at[src], ret_r.at[y],
-            device_id=at_row(src), device_id_type=MESH)
-
-    tile = dim // 4
-
-    @pl.loop(0, 5)
-    def _(b):
-        @pl.when(b < 4)
+    def giveback(src, h):
+        return pltpu.make_async_remote_copy(
+            summed.at[src, :, columns_of(h)], back.at[y, :, columns_of(h)], ret_s.at[src, h], ret_r.at[h],
+            device_id=at_row(mate), device_id_type=MESH)
+
+    def inward(b, h):
+        return pltpu.make_async_remote_copy(
+            summed.at[block(b), :, columns_of(h)], via.at[b, :, columns_of(h)], ret_s.at[block(b), h], via_r.at[b, h],
+            device_id=at_row(mate), device_id_type=MESH)
+
+    def outward(b, h):
+        return pltpu.make_async_remote_copy(
+            joined.at[b, :, columns_of(h)], given_in.at[:, columns_of(h)], join_s.at[b, h], join_r.at[h],
+            device_id=at_row(block(b)), device_id_type=MESH)
+
+    def lift(gate, hot, value, g):
+        gate = jnp.sum(jnp.where(lane == g, gate, 0.0), axis=1, keepdims=True)
+        return gate * jnp.dot(hot[:, :CAP], value, preferred_element_type=F32)
+
+    def item(i):
+        i = jnp.maximum(i, 0)
+        j = lax.rem(i, PAIR * PARTS)
+        return i // (PAIR * PARTS) * PAIR + lax.rem(j, PAIR), j // PAIR
+
+    @pl.loop(0, 4 * PARTS + LAG + JOIN)
+    def _(i):
+        @pl.when(i < 4 * PARTS)
         def _():
+            b, h = item(i)
             src = block(b)
-            relay(src).wait_recv()
-            xn = norm(1, src)
-            hid = jnp.concatenate([activate(xn, 0), activate(xn, 1)], axis=1)
-            for t in range(4):
-                cols = pl.ds(t * tile, tile)
-                mate_part[src, :, cols] = jnp.dot(hid, wd[:, cols], preferred_element_type=F32).astype(BF16)
-            partial(src).start()
-
-            @pl.when(b + EARLY < 4)
-            def _():
-                relay(block(b + EARLY)).start()
-
-            hid = hidden[src]
-            for t in range(4):
-                cols = pl.ds(t * tile, tile)
-                own_part[src, :, cols] = jnp.dot(hid, wd[:, cols], preferred_element_type=F32)
-
-        @pl.when(b > 0)
+            cols = columns_of(h)
+
+            @pl.when((h == 0) & (b > 0))
+            def _():
+                relay(src).wait_recv()
+                mate_normed[...] = norm(1, src)
+                mate_hidden[src, :, pl.ds(0, width)] = activate(mate_normed[...], 0)
+
+            @pl.when(h == 0)
+            def _():
+                mate_hidden[src, :, pl.ds(width, width)] = activate(mate_normed[...], 1)
+
+            @pl.when(b == 0)
+            def _():
+                wide(h).wait_recv()
+
+            mate_part[src, :, cols] = jnp.dot(
+                mate_hidden[src], wd[:, cols], preferred_element_type=F32).astype(BF16)
+            partial(src, h).start()
+
+            @pl.when((h == 0) & (b + SOON < 4) & jnp.logical_not(enters))
+            def _():
+                relay(block(b + SOON)).start()
+
+            @pl.when(i == 0)
+            def _():
+                own_rows(1)
+
+            own_part[src, :, cols] = jnp.dot(hidden[src], wd[:, cols], preferred_element_type=F32)
+
+        @pl.when((i >= LAG) & (i < 4 * PARTS + LAG))
         def _():
-            src = block(b - 1)
-            partial(src).wait_recv()
-            total = (own_part[src] + got_part[src].astype(F32)).astype(BF16)
-
-            @pl.when(b < 4)
-            def _():
-                summed[src] = total
-                giveback(src).start()
-
-            @pl.when(b == 4)
-            def _():
-                back[y] = total
-
-    for i in range(1, 4):
-        g = lax.rem(y + i, 4)
+            b, h = item(i - LAG)
+            src = block(b)
+            cols = columns_of(h)
+            partial(src, h).wait_recv()
+            value = (own_part[src, :, cols] + got_part[src, :, cols].astype(F32)).astype(BF16)
+
+            @pl.when(b < 3)
+            def _():
+                summed[src, :, cols] = value
+
+            @pl.when((b < 2) & jnp.logical_not(inner))
+            def _():
+                inward(b, h).start()
+
+            @pl.when(b == 2)
+            def _():
+                giveback(src, h).start()
+
+            @pl.when(b == 3)
+            def _():
+                back[y, :, cols] = value
+
+        @pl.when(inner & (i >= LAG + JOIN))
+        def _():
+            b, h = item(i - LAG - JOIN)
+
+            @pl.when(b < 2)
+            def _():
+                cols = columns_of(h)
+                inward(b, h).wait_recv()
+                gate = far_gate_of[b]
+                joined[b, :, cols] = (
+                    lift(gate, far_place[b, y], summed[block(b), :, cols], y)
+                    + lift(gate, far_place[b, mate], via[b, :, cols], mate)).astype(BF16)
+                outward(b, h).start()
+
+    for h in range(PARTS):
+        cols = pl.ds(h * tile, tile)
+        total[:, cols] = inc[:, cols].astype(F32) + lift(gate_of[...], place_t[y], back[y, :, cols], y)
+
+    for h in range(PARTS):
+        cols = pl.ds(h * tile, tile)
         pltpu.make_async_remote_copy(
-            summed.at[0], back.at[g], ret_s.at[0], ret_r.at[g],
-            device_id=at_row(g), device_id_type=MESH).wait_recv()
-
-    for t in range(4):
-        cols = pl.ds(t * tile, tile)
-        total = inc[:, cols].astype(F32)
-        for g in range(NEXP):
-            total = total + gate_of[:, g:g + 1] * jnp.dot(
-                place_t[g][:, :CAP], back[g, :, cols], preferred_element_type=F32)
-        out[:, cols] = total.astype(BF16)
+            summed.at[0, :, cols], back.at[mate, :, cols], ret_s.at[0, h], ret_r.at[h],
+            device_id=at_row(mate), device_id_type=MESH).wait_recv()
+        total[:, cols] = total[:, cols] + lift(gate_of[...], place_t[mate], back[mate, :, cols], mate)
+
+    for h in range(PARTS):
+        cols = pl.ds(h * tile, tile)
+        outward(0, h).wait_recv()
+        out[:, cols] = (total[:, cols] + given_in[:, cols].astype(F32)).astype(out.dtype)
+
+    for copy in meta:
+        copy.wait_send()
 
     for i in range(SHIFT_PARTS):
         shift(i, nxt).wait_send()
@@ -282,15 +414,34 @@
         for i in range(SHIFT_PARTS):
             second_leg(i).wait_send()
 
-    for copy in weights:
+    for copy in narrow:
         copy.wait_send()
-    for k in range(3):
-        dispatch(k).wait_send()
+    for h in range(PARTS):
+        wide(h).wait_send()
+    dispatch.wait_send()
+    for i in range(SHIFT_PARTS):
+        crossing(i, mine).wait_send()
+
+    @pl.when(inner)
+    def _():
+        for b in range(2):
+            for i in range(SHIFT_PARTS):
+                passing(b, i).wait_send()
+
     for i in range(4):
         relay(i).wait_send()
-        partial(i).wait_send()
-    for i in range(1, 4):
-        giveback(lax.rem(y + i, 4)).wait_send()
+        for h in range(PARTS):
+            partial(i, h).wait_send()
+    for h in range(PARTS):
+        giveback(mate, h).wait_send()
+        for b in range(2):
+            @pl.when(inner)
+            def _():
+                outward(b, h).wait_send()
+
+            @pl.when(jnp.logical_not(inner))
+            def _():
+                inward(b, h).wait_send()
 
 
 def local(acts, routes, gates, norm_gain, gate_w, up_w, down_w):
@@ -308,28 +459,43 @@
         scratch_shapes=[
             pltpu.VMEM((tok, dim), BF16),
             pltpu.VMEM((tok, dim), BF16),
-            pltpu.VMEM((3, CAP, dim), BF16),
+            pltpu.VMEM((CAP, dim), BF16),
+            pltpu.VMEM((2, tok, dim), BF16),
+            pltpu.VMEM((2, CAP, dim), BF16),
             pltpu.VMEM((2, 4, CAP, dim), BF16),
             pltpu.VMEM((2, dim, width), BF16),
             pltpu.VMEM((2, dim, width), BF16),
             pltpu.VMEM((2 * width, dim), BF16),
             pltpu.VMEM((4, CAP, dim), BF16),
+            pltpu.VMEM((CAP, dim), BF16),
+            pltpu.VMEM((4, CAP, 2 * width), BF16),
             pltpu.VMEM((4, CAP, 2 * width), BF16),
             pltpu.VMEM((4, CAP, dim), F32),
             pltpu.VMEM((4, CAP, dim), BF16),
             pltpu.VMEM((4, CAP, dim), BF16),
             pltpu.VMEM((4, CAP, dim), BF16),
             pltpu.VMEM((4, CAP, dim), BF16),
+            pltpu.VMEM((2, CAP, dim), BF16),
+            pltpu.VMEM((2, tok, dim), BF16),
+            pltpu.VMEM((tok, dim), BF16),
+            pltpu.VMEM((tok, dim), F32),
             pltpu.VMEM((4, tok, tok), BF16),
             pltpu.VMEM((4, tok, tok), BF16),
             pltpu.VMEM((tok, tok), F32),
+            pltpu.VMEM((2, 2, tok), jnp.int32),
+            pltpu.VMEM((2, 2, tok), F32),
+            pltpu.VMEM((2, 4, tok, tok), BF16),
+            pltpu.VMEM((2, 4, tok, tok), BF16),
+            pltpu.VMEM((2, tok, tok), F32),
             dma((SHIFT_PARTS,)), dma((SHIFT_PARTS,)),
             dma((SHIFT_PARTS,)), dma((SHIFT_PARTS,)),
-            dma((3,)), dma((3,)), dma((3,)),
-            dma((3,)), dma((4,)),
+            dma((2 + PARTS,)), dma((2 + PARTS,)), dma((3,)),
+            dma((1,)), dma((4,)),
             dma((4,)), dma((4,)),
-            dma((4,)), dma((4,)),
-            dma((4,)), dma((4,)),
+            dma((4, PARTS)), dma((4, PARTS)),
+            dma((4, PARTS)), dma((PARTS,)),
+            dma((2, PARTS)), dma((2, PARTS)), dma((PARTS,)), dma((2,)), dma((2, 2)),
+            dma((SHIFT_PARTS,)), dma((2, SHIFT_PARTS)), dma((2, SHIFT_PARTS)),
         ],
         compiler_params=pltpu.CompilerParams(
             collective_id=0, has_side_effects=True, vmem_limit_bytes=56 * 1024 * 1024),

time: 97.4 us -> 97.1 us (level)
  no operation moved by 1% of the time
where the time goes in v3:
time: 97.1 us; the launch traced here: 96.9 us
  Pallas kernels  95 us (98%)
  local copies, waits for them, and re-layouts  1.88 us (2%)
    pallas_call x1, Pallas kernels, local(): pl.pallas_call(kernel, name='relay_experts', out_shape=jax.ShapeDtypeStru...  95 us

profile of v3, /device:TPU:10, one launch (start us, length us, event | category | flops | bytes accessed | tf_op | source)
XLA Modules:
  0.0 96.9 jit_solution(18418366515873503762)
XLA Ops:
  0.0 95.0 %relay_experts.1 = bf16[128,2048]{1,0:T(8,128)(2,1)} custom-call(bf16[128,2048]{1,0:T(8,128)(2,1)} %bitcast.15, s32[2,128]{1,0:T(2,128)} %bitcast.16, f32[2,128]{1,0:T(2,128)} %bitcast.17, f32[1,2048]{1,0:T(1,128)} %gain.1, bf16[2048,256]{1,0:T(8,128)(2,1)} %bitcast.12, bf16[2048,256]{1,0:T(8,128)(2,1)} %bitcast.13, bf16[256,2048]{1,0:T(8,128)(2,1)} %bitcast.14), custom_call_target="tpu_custom_call" | custom-call | tf_op jit(solution)/shard_map/relay_experts/pallas_call | solution.py:453
  95.0 1.9 %copy.9 = bf16[1,128,2048]{2,1,0:T(8,128)(2,1)} copy(bf16[1,128,2048]{2,1,0:T(8,128)(2,1)} %bitcast.11) | data formatting | bytes 1048576

commit v4 on v3

--- a/solution.py
+++ b/solution.py
@@ -15,7 +15,7 @@
 PARTS = 2
 PAIR = 1
 LAG = 2
-JOIN = 1
+JOIN = 2
 MESH = pl.DeviceIdType.MESH
 F32 = jnp.float32
 BF16 = jnp.bfloat16
@@ -31,10 +31,10 @@
 
 def kernel(
     acts, routes, gates, gain, gate_w, up_w, down_w, out,
-    inc, hop, packs, far_rows, onward, rows, wg, wu, wd, normed, mate_normed, hidden, mate_hidden, own_part, mate_part, got_part,
-    summed, back, via, joined, given_in, total, place_t, place, gate_of, far_routes, far_gates, far_place, far_pick, far_gate_of,
+    inc, hop, packs, rows, wg, wu, wd, normed, mate_normed, hidden, mate_hidden, own_part, mate_part, got_part,
+    summed, back, via, joined, given_in, total, place_t, place, gate_of, far_routes, far_gates, far_place, far_gate_of,
     shift_s, shift_r, hop_s, hop_r, w_s, w_r, w_l, y_s, y_r, rel_s, rel_r, part_s, part_r, ret_s, ret_r,
-    via_r, join_s, join_r, meta_s, meta_r, far_s, far_r, on_s,
+    via_r, join_s, join_r, meta_s, meta_r,
 ):
     tok, dim = inc.shape
     width = gate_w.shape[1]
@@ -177,27 +177,20 @@
     def packed(g, cols):
         return jnp.dot(place[g][:CAP], inc[:, cols], preferred_element_type=F32).astype(BF16)
 
-    def crossing(i, to):
-        return pltpu.make_async_remote_copy(
-            inc.at[:, columns[i]], far_rows.at[to, :, columns[i]], far_s.at[i], far_r.at[to, i],
-            device_id=at_row(across), device_id_type=MESH)
-
     for i in range(SHIFT_PARTS):
         shift(i, nxt).wait_recv()
         cols = columns[i]
-        crossing(i, mine).start()
-        packs[:, cols] = packed(mate, cols)
+        for k in range(3):
+            packs[k, :, cols] = packed(far_order(y, k), cols)
         rows[0, y, :, cols] = packed(y, cols)
 
-    dispatch = pltpu.make_async_remote_copy(
-        packs, rows.at[0, y], y_s.at[0], y_r.at[y], device_id=at_row(mate), device_id_type=MESH)
-    dispatch.start()
-
-    def passing(b, i):
-        src = far_order(y, b)
-        return pltpu.make_async_remote_copy(
-            onward.at[b, :, columns[i]], rows.at[0, src, :, columns[i]], on_s.at[b, i], y_r.at[src],
-            device_id=at_row(mate), device_id_type=MESH)
+    def dispatch(k):
+        return pltpu.make_async_remote_copy(
+            packs.at[k], rows.at[0, y], y_s.at[k], y_r.at[y],
+            device_id=at_row(far_order(y, k)), device_id_type=MESH)
+
+    for k in range(3):
+        dispatch(k).start()
 
     @pl.when(inner)
     def _():
@@ -208,22 +201,12 @@
                     device_id_type=MESH).wait_recv()
             far_gate_of[i], far_hots = table(far_routes[i], far_gates[i])
             for g in range(NEXP):
-                far_pick[i, g] = far_hots[g].astype(BF16)
                 far_place[i, g] = far_hots[g].T.astype(BF16)
-        for i in range(SHIFT_PARTS):
-            for b in range(2):
-                crossing(i, b).wait_recv()
-                value = far_rows[b, :, columns[i]]
-                onward[b, :, columns[i]] = jnp.dot(
-                    far_pick[b, mate][:CAP], value, preferred_element_type=F32).astype(BF16)
-                passing(b, i).start()
-                rows[0, far_order(y, b), :, columns[i]] = jnp.dot(
-                    far_pick[b, y][:CAP], value, preferred_element_type=F32).astype(BF16)
 
     def arrival(src):
         return pltpu.make_async_remote_copy(
-            packs, rows.at[0, src], y_s.at[0], y_r.at[src],
-            device_id=at_row(mate), device_id_type=MESH)
+            packs.at[0], rows.at[0, src], y_s.at[0], y_r.at[src],
+            device_id=at_row(src), device_id_type=MESH)
 
     def relay(src):
         return pltpu.make_async_remote_copy(
@@ -252,10 +235,7 @@
     @pl.loop(0, 3)
     def _(b):
         src = block(b)
-
-        @pl.when((b == 2) | jnp.logical_not(inner))
-        def _():
-            arrival(src).wait_recv()
+        arrival(src).wait_recv()
 
         @pl.when((b < EARLY) | enters)
         def _():
@@ -418,16 +398,8 @@
         copy.wait_send()
     for h in range(PARTS):
         wide(h).wait_send()
-    dispatch.wait_send()
-    for i in range(SHIFT_PARTS):
-        crossing(i, mine).wait_send()
-
-    @pl.when(inner)
-    def _():
-        for b in range(2):
-            for i in range(SHIFT_PARTS):
-                passing(b, i).wait_send()
-
+    for k in range(3):
+        dispatch(k).wait_send()
     for i in range(4):
         relay(i).wait_send()
         for h in range(PARTS):
@@ -459,9 +431,7 @@
         scratch_shapes=[
             pltpu.VMEM((tok, dim), BF16),
             pltpu.VMEM((tok, dim), BF16),
-            pltpu.VMEM((CAP, dim), BF16),
-            pltpu.VMEM((2, tok, dim), BF16),
-            pltpu.VMEM((2, CAP, dim), BF16),
+            pltpu.VMEM((3, CAP, dim), BF16),
             pltpu.VMEM((2, 4, CAP, dim), BF16),
             pltpu.VMEM((2, dim, width), BF16),
             pltpu.VMEM((2, dim, width), BF16),
@@ -485,17 +455,15 @@
             pltpu.VMEM((2, 2, tok), jnp.int32),
             pltpu.VMEM((2, 2, tok), F32),
             pltpu.VMEM((2, 4, tok, tok), BF16),
-            pltpu.VMEM((2, 4, tok, tok), BF16),
             pltpu.VMEM((2, tok, tok), F32),
             dma((SHIFT_PARTS,)), dma((SHIFT_PARTS,)),
             dma((SHIFT_PARTS,)), dma((SHIFT_PARTS,)),
             dma((2 + PARTS,)), dma((2 + PARTS,)), dma((3,)),
-            dma((1,)), dma((4,)),
+            dma((3,)), dma((4,)),
             dma((4,)), dma((4,)),
             dma((4, PARTS)), dma((4, PARTS)),
             dma((4, PARTS)), dma((PARTS,)),
             dma((2, PARTS)), dma((2, PARTS)), dma((PARTS,)), dma((2,)), dma((2, 2)),
-            dma((SHIFT_PARTS,)), dma((2, SHIFT_PARTS)), dma((2, SHIFT_PARTS)),
         ],
         compiler_params=pltpu.CompilerParams(
             collective_id=0, has_side_effects=True, vmem_limit_bytes=56 * 1024 * 1024),

time: 97.1 us -> 94.8 us (0.976)
  Pallas kernels: 95 us -> 92.7 us
    pallas_call x1, Pallas kernels: 95 us -> 92.7 us  [local(): pl.pallas_call(kernel, name='relay_experts', out_shape=jax.ShapeDtypeStru...]
where the time goes in v4:
time: 94.8 us; the launch traced here: 94.6 us
  Pallas kernels  92.7 us (98%)
  local copies, waits for them, and re-layouts  1.88 us (2%)
    pallas_call x1, Pallas kernels, local(): pl.pallas_call(kernel, name='relay_experts', out_shape=jax.ShapeDtypeStru...  92.7 us

profile of v4, /device:TPU:10, one launch (start us, length us, event | category | flops | bytes accessed | tf_op | source)
XLA Modules:
  0.0 94.6 jit_solution(13321215542549600674)
XLA Ops:
  0.0 92.7 %relay_experts.1 = bf16[128,2048]{1,0:T(8,128)(2,1)} custom-call(bf16[128,2048]{1,0:T(8,128)(2,1)} %bitcast.15, s32[2,128]{1,0:T(2,128)} %bitcast.16, f32[2,128]{1,0:T(2,128)} %bitcast.17, f32[1,2048]{1,0:T(1,128)} %gain.1, bf16[2048,256]{1,0:T(8,128)(2,1)} %bitcast.12, bf16[2048,256]{1,0:T(8,128)(2,1)} %bitcast.13, bf16[256,2048]{1,0:T(8,128)(2,1)} %bitcast.14), custom_call_target="tpu_custom_call" | custom-call | tf_op jit(solution)/shard_map/relay_experts/pallas_call | solution.py:425
  92.7 1.9 %copy.9 = bf16[1,128,2048]{2,1,0:T(8,128)(2,1)} copy(bf16[1,128,2048]{2,1,0:T(8,128)(2,1)} %bitcast.11) | data formatting | bytes 1048576

commit v5 on v4

--- a/solution.py
+++ b/solution.py
@@ -177,20 +177,18 @@
     def packed(g, cols):
         return jnp.dot(place[g][:CAP], inc[:, cols], preferred_element_type=F32).astype(BF16)
 
+    def dispatch(k, i):
+        return pltpu.make_async_remote_copy(
+            packs.at[k, :, columns[i]], rows.at[0, y, :, columns[i]], y_s.at[k, i], y_r.at[y],
+            device_id=at_row(far_order(y, k)), device_id_type=MESH)
+
     for i in range(SHIFT_PARTS):
         shift(i, nxt).wait_recv()
         cols = columns[i]
         for k in range(3):
             packs[k, :, cols] = packed(far_order(y, k), cols)
+            dispatch(k, i).start()
         rows[0, y, :, cols] = packed(y, cols)
-
-    def dispatch(k):
-        return pltpu.make_async_remote_copy(
-            packs.at[k], rows.at[0, y], y_s.at[k], y_r.at[y],
-            device_id=at_row(far_order(y, k)), device_id_type=MESH)
-
-    for k in range(3):
-        dispatch(k).start()
 
     @pl.when(inner)
     def _():
@@ -205,7 +203,7 @@
 
     def arrival(src):
         return pltpu.make_async_remote_copy(
-            packs.at[0], rows.at[0, src], y_s.at[0], y_r.at[src],
+            packs.at[0], rows.at[0, src], y_s.at[0, 0], y_r.at[src],
             device_id=at_row(src), device_id_type=MESH)
 
     def relay(src):
@@ -399,7 +397,8 @@
     for h in range(PARTS):
         wide(h).wait_send()
     for k in range(3):
-        dispatch(k).wait_send()
+        for i in range(SHIFT_PARTS):
+            dispatch(k, i).wait_send()
     for i in range(4):
         relay(i).wait_send()
         for h in range(PARTS):
@@ -459,7 +458,7 @@
             dma((SHIFT_PARTS,)), dma((SHIFT_PARTS,)),
             dma((SHIFT_PARTS,)), dma((SHIFT_PARTS,)),
             dma((2 + PARTS,)), dma((2 + PARTS,)), dma((3,)),
-            dma((3,)), dma((4,)),
+            dma((3, SHIFT_PARTS)), dma((4,)),
             dma((4,)), dma((4,)),
             dma((4, PARTS)), dma((4, PARTS)),
             dma((4, PARTS)), dma((PARTS,)),

time: 94.8 us -> 94 us (level)
  no operation moved by 1% of the time
where the time goes in v5:
time: 94 us; the launch traced here: 93.7 us
  Pallas kernels  91.9 us (98%)
  local copies, waits for them, and re-layouts  1.88 us (2%)
    pallas_call x1, Pallas kernels, local(): pl.pallas_call(kernel, name='relay_experts', out_shape=jax.ShapeDtypeStru...  91.9 us
    unnamed x1, local copies, waits for them, and re-layouts  1.88 us

profile of v5, /device:TPU:10, one launch (start us, length us, event | category | flops | bytes accessed | tf_op | source)
XLA Modules:
  0.0 93.7 jit_solution(4215787808588969710)
XLA Ops:
  0.0 91.9 %relay_experts.1 = bf16[128,2048]{1,0:T(8,128)(2,1)} custom-call(bf16[128,2048]{1,0:T(8,128)(2,1)} %bitcast.15, s32[2,128]{1,0:T(2,128)} %bitcast.16, f32[2,128]{1,0:T(2,128)} %bitcast.17, f32[1,2048]{1,0:T(1,128)} %gain.1, bf16[2048,256]{1,0:T(8,128)(2,1)} %bitcast.12, bf16[2048,256]{1,0:T(8,128)(2,1)} %bitcast.13, bf16[256,2048]{1,0:T(8,128)(2,1)} %bitcast.14), custom_call_target="tpu_custom_call" | custom-call | tf_op jit(solution)/shard_map/relay_experts/pallas_call | solution.py:424
  91.9 1.9 %copy.9 = bf16[1,128,2048]{2,1,0:T(8,128)(2,1)} copy(bf16[1,128,2048]{2,1,0:T(8,128)(2,1)} %bitcast.11) | data formatting | bytes 1048576
